TPU v7x, 32 devices: a whole 2x2x4 slice. The times are simulated.
32 devices in a mesh: tm: 4 (over z), feat: 8 (over y, x, core).
Axes of the slice: x: 2, y: 2, z: 4, core: 2. Of those that a mesh axis runs over, the one named last changes fastest.
Arguments:
- trajectory: float32 [16384, 2048], P('tm', 'feat'), may hold values from -8 to 9
Outputs:
- moments: float32 [4, 2048, 2048], P(None, 'feat', 'tm')
All inputs are finite; a program needn't handle non-finite values.
Results may differ from a plain program's by a relative error of at most 0.00035.
Values may be sent and summed in bfloat16 or wider, within the bound.
No kernel may reach another device: no remote copies, remote signals or barrier semaphores. Data moves between devices by JAX's collectives and lax.ppermute only.
A program may use at most 128 MiB of HBM per device.

v0:
```python
import jax
import jax.numpy as jnp
from jax import lax
from jax.sharding import PartitionSpec as P

HALO = 16
lag_values = (0, 1, 4, 16)


def passed_along(value, axis, steps):
    count = lax.axis_size(axis)
    initial, last = (max(0, -steps), min(count, count - steps))
    return lax.ppermute(value, axis, [(source, source + steps) for source in range(initial, last)])


def shards(trajectory):
    rows = trajectory.shape[0]
    frames = rows * lax.axis_size("tm")
    total = lax.psum(jnp.sum(trajectory, axis=0), "tm")
    mean = total / frames
    centered = (trajectory - mean).astype(jnp.bfloat16)
    gathered = lax.all_gather(centered, "feat", axis=1, tiled=True)
    tail = passed_along(gathered[:HALO], "tm", -1)
    extended = jnp.concatenate([gathered, tail], axis=0)
    blocks = [
        lax.dot_general(
            centered,
            extended[lag : lag + rows],
            (((0,), (0,)), ((), ())),
            preferred_element_type=jnp.float32,
        )
        for lag in lag_values
    ]
    partial_sum = jnp.stack(blocks)
    summed = lax.psum_scatter(partial_sum, "tm", scatter_dimension=2, tiled=True)
    scales = jnp.sqrt(jnp.float32(frames) - jnp.array(lag_values, jnp.float32))
    return summed / scales[:, None, None]


def solution(mesh):
    placed = (P("tm", "feat"),)
    return jax.shard_map(
        shards, mesh=mesh, in_specs=placed, out_specs=P(None, "feat", "tm"), check_vma=False
    )
```

profile of v0, /device:TPU:0, one launch (start us, length us, event | category | flops | bytes accessed | tf_op | source)
XLA Modules:
  0.0 323.2 jit_solution(11681123390294850944)
XLA Ops:
  6.5 0.0 all-gather.2.cloned.1.call-start
  6.5 2.7 reduce_sum.9
  9.3 13.5 %psum.7 = f32[256]{0:T(256)S(1)} all-reduce(f32[256]{0:T(256)S(1)} %reduce_sum.9), channel_id=1, replica_groups=mesh['tm'=4,'feat'=8] {'tm'}, use_global_device_ids=true, to_apply=%region_1.0 | all-reduce | flops 256 | bytes 2048 | tf_op jit(solution)/shard_map/psum | solution.py:19
  22.8 3.9 %subtract_convert_fusion = bf16[4096,256]{1,0:T(8,128)(2,1)} fusion(f32[4096,256]{1,0:T(8,128)} %param.2, f32[256]{0:T(256)S(1)} %broadcast_multiply_fusion.1), kind=kLoop, calls=%fused_computation.7 | loop fusion | flops 2097152 | bytes 6292480 | tf_op jit(solution)/shard_map/convert_element_type | solution.py:21
  26.6 0.0 all-gather.2.cloned.1.call-update
  26.7 0.0 reduce-scatter.2.cloned.1.call-start
  26.7 91.3 %all-gather.2.cloned.1.call-done = bf16[4096,2048]{1,0:T(8,128)(2,1)} async-done(((bf16[4096,256]{1,0:T(8,128)(2,1)}), bf16[4096,2048]{1,0:T(8,128)(2,1)}) %all-gather.2.cloned.1.call-update) | async-done | bytes 16777232 | tf_op jit(solution)/shard_map/all_gather | solution.py:22
  118.0 0.8 slice.16
  118.9 1.3 collective-permute-start
  120.2 0.0 copy-start
  120.2 8.9 %convolution_bitcast_fusion = f32[1,256,2048]{2,1,0:T(8,128)S(1)} fusion(bf16[4096,256]{1,0:T(8,128)(2,1)} %subtract_convert_fusion, bf16[4096,2048]{1,0:T(8,128)(2,1)} %all-gather.2.cloned.1.call-done), kind=kOutput, calls=%fused_computation.11 | convolution fusion | flops 4294967296 | bytes 20971520 | tf_op jit(solution)/shard_map/dot_general | solution.py:26
  129.1 2.2 copy-done
  131.3 0.0 copy-start.1
  131.3 7.0 %constant_dynamic-update-slice_fusion.1 = bf16[4112,2048]{1,0:T(8,128)(2,1)} fusion(bf16[4096,2048]{1,0:T(8,128)(2,1)S(1)} %copy-done), kind=kLoop, calls=%fused_computation.14 | loop fusion | bytes 33554432
  138.3 0.0 collective-permute-done
  138.3 0.6 constant_dynamic-update-slice_fusion
  138.9 0.0 copy-done.1
  138.9 8.2 %fusion.12 = f32[1,256,2048]{2,1,0:T(8,128)S(1)} fusion(bf16[4096,256]{1,0:T(8,128)(2,1)S(1)} %copy-done.1, bf16[4112,2048]{1,0:T(8,128)(2,1)} %constant_dynamic-update-slice_fusion), kind=kOutput, calls=%fused_computation.10 | convolution fusion | flops 4294967296 | bytes 20971520 | tf_op jit(solution)/shard_map/dot_general | solution.py:26
  147.1 8.2 %fusion.9 = f32[1,256,2048]{2,1,0:T(8,128)S(1)} fusion(bf16[4096,256]{1,0:T(8,128)(2,1)S(1)} %copy-done.1, bf16[4112,2048]{1,0:T(8,128)(2,1)} %constant_dynamic-update-slice_fusion), kind=kOutput, calls=%fused_computation.9 | convolution fusion | flops 4294967296 | bytes 20971520 | tf_op jit(solution)/shard_map/dot_general | solution.py:26
  155.3 8.2 %fusion.6 = f32[1,256,2048]{2,1,0:T(8,128)S(1)} fusion(bf16[4096,256]{1,0:T(8,128)(2,1)S(1)} %copy-done.1, bf16[4112,2048]{1,0:T(8,128)(2,1)} %constant_dynamic-update-slice_fusion), kind=kOutput, calls=%fused_computation.8 | convolution fusion | flops 4294967296 | bytes 20971520 | tf_op jit(solution)/shard_map/dot_general | solution.py:26
  163.5 3.7 %pad_maximum_fusion = f32[4,256,2048]{2,1,0:T(8,128)} fusion(f32[1,256,2048]{2,1,0:T(8,128)S(1)} %fusion.12, f32[1,256,2048]{2,1,0:T(8,128)S(1)} %fusion.9, f32[1,256,2048]{2,1,0:T(8,128)S(1)} %fusion.6, f32[1,256,2048]{2,1,0:T(8,128)S(1)} %convolution_bitcast_fusion), kind=kLoop, calls=%fused_computation.6 | loop fusion | flops 6291456 | bytes 16777216 | tf_op jit(solution)/shard_map/stack | solution.py:34
  167.2 0.0 copy-start.2
  167.2 0.0 reduce-scatter.2.cloned.1.call-update
  167.2 145.9 %reduce-scatter.2.cloned.1.call-done = f32[4,256,512]{2,1,0:T(8,128)} async-done(((f32[4,256,2048]{2,1,0:T(8,128)}), f32[4,256,512]{2,1,0:T(8,128)}) %reduce-scatter.2.cloned.1.call-update) | async-done | bytes 2097168 | tf_op jit(solution)/shard_map/reduce_scatter | solution.py:35
  313.1 0.0 copy-done.2
  313.1 3.3 %broadcast_multiply_fusion = f32[4,256,512]{2,1,0:T(8,128)} fusion(f32[4,256,512]{2,1,0:T(8,128)} %reduce-scatter.2.cloned.1.call-done, f32[4]{0:T(128)S(1)} %copy-done.2), kind=kLoop, calls=%fused_computation.12 | loop fusion | flops 524288 | bytes 4194320 | tf_op jit(solution)/shard_map/div | solution.py:37
  (1 shorter events, 0.0 us)
Async XLA Ops:
  6.5 111.5 %all-gather.2.cloned.1.call-start = ((), (), s32[]{:S(2)}) async-start(), calls=%async_computation.1 | async-start | bytes 18874368 | tf_op jit(solution)/shard_map/all_gather | solution.py:22
  26.7 286.4 %reduce-scatter.2.cloned.1.call-start = ((), (), s32[]{:S(2)}) async-start(), calls=%async_computation.2 | async-start | bytes 10485760 | tf_op jit(solution)/shard_map/reduce_scatter | solution.py:35
  118.9 19.4 %collective-permute-start = (bf16[16,2048]{1,0:T(8,128)(2,1)S(1)}, bf16[16,2048]{1,0:T(8,128)(2,1)S(1)}, u32[]{:S(2)}, u32[]{:S(2)}) collective-permute-start(bf16[16,2048]{1,0:T(8,128)(2,1)S(1)} %slice.16), channel_id=1, source_target_pairs={{8,0},{16,8},{24,16},{9,1},{17,9},{25,17},{10,2},{18,10},{26,18},{... | collective-permute-start | bytes 196616 | tf_op jit(solution)/shard_map/ppermute | solution.py:13
  120.2 11.1 %copy-start = (bf16[4096,2048]{1,0:T(8,128)(2,1)S(1)}, bf16[4096,2048]{1,0:T(8,128)(2,1)}, u32[]{:S(2)}) copy-start(bf16[4096,2048]{1,0:T(8,128)(2,1)} %all-gather.2.cloned.1.call-done) | copy-start | bytes 50331652
  131.3 7.6 %copy-start.1 = (bf16[4096,256]{1,0:T(8,128)(2,1)S(1)}, bf16[4096,256]{1,0:T(8,128)(2,1)}, u32[]{:S(2)}) copy-start(bf16[4096,256]{1,0:T(8,128)(2,1)} %subtract_convert_fusion) | copy-start | bytes 6291460
  167.2 145.9 %copy-start.2 = (f32[4]{0:T(128)S(1)}, f32[4]{0:T(128)}, u32[]{:S(2)}) copy-start(f32[4]{0:T(128)} %constant.13) | copy-start | bytes 52
Sparse Core Ops, SparseCore 0:
  26.8 91.2 all-gather.1
  167.3 145.7 reduce-scatter.1
where the time goes:
time: 324 us; the launch traced here: 323 us
  waiting for transfers between devices  237 us (73%)
  matrix products  33.5 us (10%)
  other arithmetic  13.5 us (4%)
  blocking collectives  13.5 us (4%)
  between operations  13.5 us (4%)
  local copies, waits for them, and re-layouts  10.7 us (3%)
    reduce_scatter x1, waiting for transfers between devices, shards(): lax.psum_scatter(partial_sum, 'tm', scatter_dimension=2, tiled=True)  146 us
    all_gather x1, waiting for transfers between devices, shards(): gathered = lax.all_gather(centered, 'feat', axis=1, tiled=True)  91.3 us
    dot_general x4, matrix products, shards(): lax.dot_general(centered, extended[lag:lag + rows], (((0,), (0,)), ((), (...  33.5 us
    psum x1, blocking collectives, shards(): total = lax.psum(jnp.sum(trajectory, axis=0), 'tm')  13.5 us
    unnamed x7, local copies, waits for them, and re-layouts  9.21 us
  transfers between devices with their start and end apart: 3, of which 2 were waited for; matrix products, arithmetic and copies ran while one was open for 5% of the time, Pallas kernels for 0%

commit v1 on v0

--- a/solution.py
+++ b/solution.py
@@ -19,7 +19,12 @@
     total = lax.psum(jnp.sum(trajectory, axis=0), "tm")
     mean = total / frames
     centered = (trajectory - mean).astype(jnp.bfloat16)
-    gathered = lax.all_gather(centered, "feat", axis=1, tiled=True)
+    ring = [centered]
+    for hop in range(7):
+        ring.append(lax.ppermute(ring[-1], "feat", [(dev, (dev + 1) % 8) for dev in range(8)]))
+    gathered = jnp.roll(
+        jnp.concatenate(ring[::-1], axis=1), (lax.axis_index("feat") + 1) * ring[0].shape[1], axis=1
+    )
     tail = passed_along(gathered[:HALO], "tm", -1)
     extended = jnp.concatenate([gathered, tail], axis=0)
     blocks = [

time: 324 us -> 455 us (1.40)
  waiting for transfers between devices: 237 us -> 327 us
  local copies, waits for them, and re-layouts: 10.7 us -> 49.8 us
    ppermute x0 -> x7, waiting for transfers between devices: none -> 185 us  [shards(): lax.ppermute(ring[-1], 'feat', [(dev, (dev + 1) % 8) for dev in range(8)])]
    all_gather x1 -> x0, waiting for transfers between devices: 91.3 us -> none  [shards(): gathered = lax.all_gather(centered, 'feat', axis=1, tiled=True)]
    unnamed x7 -> x40, local copies, waits for them, and re-layouts: 9.21 us -> 40.4 us
    dynamic_slice x0 -> x1, local copies, waits for them, and re-layouts: none -> 8.48 us  [shards(): jnp.roll(jnp.concatenate(ring[::-1], axis=1), (lax.axis_index('feat') + 1...]
  transfers between devices with their start and end apart: 3 -> 9, of which waited for: 2 -> 8; matrix products, arithmetic and copies ran while one was open for 5% -> 1% of each run, Pallas kernels for 0% -> 0%
where the time goes in v1:
time: 455 us
  waiting for transfers between devices  327 us (72%)
  local copies, waits for them, and re-layouts  49.8 us (11%)
  matrix products  32.1 us (7%)
  other arithmetic  17.1 us (4%)
  blocking collectives  13.5 us (3%)
  between operations  13.5 us (3%)
    ppermute x7, waiting for transfers between devices, shards(): lax.ppermute(ring[-1], 'feat', [(dev, (dev + 1) % 8) for dev in range(8)])  185 us
    reduce_scatter x1, waiting for transfers between devices, shards(): lax.psum_scatter(partial_sum, 'tm', scatter_dimension=2, tiled=True)  142 us
    unnamed x40, local copies, waits for them, and re-layouts  40.4 us
    dot_general x4, matrix products, shards(): lax.dot_general(centered, extended[lag:lag + rows], (((0,), (0,)), ((), (...  32.1 us
    psum x1, blocking collectives, shards(): total = lax.psum(jnp.sum(trajectory, axis=0), 'tm')  13.5 us
  transfers between devices with their start and end apart: 9, of which 8 were waited for; matrix products, arithmetic and copies ran while one was open for 1% of the time, Pallas kernels for 0%

profile of v1, /device:TPU:0, one launch (start us, length us, event | category | flops | bytes accessed | tf_op | source)
XLA Modules:
  0.0 454.5 jit_solution(10431549818519657696)
XLA Ops:
  6.5 0.0 reduce-scatter.2.cloned.1.call-start
  6.5 2.7 reduce_sum.9
  9.3 13.5 %psum.7 = f32[256]{0:T(256)S(1)} all-reduce(f32[256]{0:T(256)S(1)} %reduce_sum.9), channel_id=1, replica_groups=mesh['tm'=4,'feat'=8] {'tm'}, use_global_device_ids=true, to_apply=%region_1.0 | all-reduce | flops 256 | bytes 2048 | tf_op jit(solution)/shard_map/psum | solution.py:19
  22.8 2.5 subtract_convert_fusion
  25.3 0.1 collective-permute-start
  25.4 26.3 %collective-permute-done = bf16[4096,256]{1,0:T(8,128)(2,1)S(1)} collective-permute-done((bf16[4096,256]{1,0:T(8,128)(2,1)S(1)}, bf16[4096,256]{1,0:T(8,128)(2,1)S(1)}, u32[]{:S(2)}, u32[]{:S(2)}) %collective-permute-start) | collective-permute-done | bytes 2097184 | tf_op jit(solution)/shard_map/ppermute | solution.py:24
  51.7 0.0 copy-start.2
  51.7 1.3 copy-done.2
  53.1 0.0 collective-permute-start.1
  53.1 26.4 %collective-permute-done.1 = bf16[4096,256]{1,0:T(8,128)(2,1)S(1)} collective-permute-done((bf16[4096,256]{1,0:T(8,128)(2,1)S(1)}, bf16[4096,256]{1,0:T(8,128)(2,1)S(1)}, u32[]{:S(2)}, u32[]{:S(2)}) %collective-permute-start.1) | collective-permute-done | bytes 2097184 | tf_op jit(solution)/shard_map/ppermute | solution.py:24
  79.4 0.0 copy-start.4
  79.4 1.4 copy-done.4
  80.8 0.0 collective-permute-start.2
  80.8 26.4 %collective-permute-done.2 = bf16[4096,256]{1,0:T(8,128)(2,1)S(1)} collective-permute-done((bf16[4096,256]{1,0:T(8,128)(2,1)S(1)}, bf16[4096,256]{1,0:T(8,128)(2,1)S(1)}, u32[]{:S(2)}, u32[]{:S(2)}) %collective-permute-start.2) | collective-permute-done | bytes 2097184 | tf_op jit(solution)/shard_map/ppermute | solution.py:24
  107.2 0.0 copy-start.6
  107.2 1.3 copy-done.6
  108.5 0.0 collective-permute-start.3
  108.5 26.4 %collective-permute-done.3 = bf16[4096,256]{1,0:T(8,128)(2,1)S(1)} collective-permute-done((bf16[4096,256]{1,0:T(8,128)(2,1)S(1)}, bf16[4096,256]{1,0:T(8,128)(2,1)S(1)}, u32[]{:S(2)}, u32[]{:S(2)}) %collective-permute-start.3) | collective-permute-done | bytes 2097184 | tf_op jit(solution)/shard_map/ppermute | solution.py:24
  134.8 1.3 copy-done.8
  136.1 0.0 collective-permute-start.4
  136.1 26.4 %collective-permute-done.4 = bf16[4096,256]{1,0:T(8,128)(2,1)S(1)} collective-permute-done((bf16[4096,256]{1,0:T(8,128)(2,1)S(1)}, bf16[4096,256]{1,0:T(8,128)(2,1)S(1)}, u32[]{:S(2)}, u32[]{:S(2)}) %collective-permute-start.4) | collective-permute-done | bytes 2097184 | tf_op jit(solution)/shard_map/ppermute | solution.py:24
  162.5 1.3 copy-done.10
  163.8 0.0 collective-permute-start.5
  163.8 26.5 %collective-permute-done.5 = bf16[4096,256]{1,0:T(8,128)(2,1)} collective-permute-done((bf16[4096,256]{1,0:T(8,128)(2,1)S(1)}, bf16[4096,256]{1,0:T(8,128)(2,1)}, u32[]{:S(2)}, u32[]{:S(2)}) %collective-permute-start.5) | collective-permute-done | bytes 2097184 | tf_op jit(solution)/shard_map/ppermute | solution.py:24
  190.3 0.0 collective-permute-start.6
  190.3 0.0 copy-start.1
  190.3 26.6 %collective-permute-done.6 = bf16[4096,256]{1,0:T(8,128)(2,1)} collective-permute-done((bf16[4096,256]{1,0:T(8,128)(2,1)}, bf16[4096,256]{1,0:T(8,128)(2,1)}, u32[]{:S(2)}, u32[]{:S(2)}) %collective-permute-start.6) | collective-permute-done | bytes 2097184 | tf_op jit(solution)/shard_map/ppermute | solution.py:24
  217.0 3.1 constant_dynamic-update-slice_fusion.15
  220.0 3.1 constant_dynamic-update-slice_fusion.14
  223.1 3.1 constant_dynamic-update-slice_fusion.13
  226.2 3.2 constant_dynamic-update-slice_fusion.12
  229.5 0.0 copy-done.7
  229.5 1.5 constant_dynamic-update-slice_fusion.11
  231.0 0.0 copy-done.5
  231.0 1.4 constant_dynamic-update-slice_fusion.10
  232.4 0.0 copy-done.3
  232.4 1.5 constant_dynamic-update-slice_fusion.9
  233.9 0.0 copy-done.1
  233.9 1.7 constant_dynamic-update-slice_fusion.8
  235.6 3.1 constant_dynamic-update-slice_fusion.7
  238.7 3.1 constant_dynamic-update-slice_fusion.6
  241.7 0.0 copy-done.11
  241.7 1.5 constant_dynamic-update-slice_fusion.5
  243.2 0.0 copy-done.9
  243.2 1.5 constant_dynamic-update-slice_fusion.4
  244.7 1.5 constant_dynamic-update-slice_fusion.3
  246.2 1.5 constant_dynamic-update-slice_fusion.2
  247.7 1.5 constant_dynamic-update-slice_fusion.1
  249.2 1.8 constant_dynamic-update-slice_fusion
  250.9 8.5 %constant_dynamic-slice_fusion.1 = bf16[4096,2048]{1,0:T(8,128)(2,1)S(1)} fusion(bf16[4096,4096]{1,0:T(8,128)(2,1)} %constant_dynamic-update-slice_fusion, s32[]{:T(128)S(6)} %select_n.14), kind=kLoop, calls=%fused_computation.35 | loop fusion | bytes 33554436 | tf_op jit(solution)/shard_map/jit(_roll_dynamic)/dynamic_slice | solution.py:25
  259.4 0.0 copy-start
  259.4 0.9 constant_dynamic-slice_fusion
  260.4 1.5 collective-permute-start.7
  261.8 3.3 copy-done
  265.1 4.5 convolution_bitcast_fusion
  269.7 0.0 collective-permute-done.7
  269.7 9.2 %fusion.13 = f32[1,256,2048]{2,1,0:T(8,128)S(1)} fusion(bf16[4096,256]{1,0:T(8,128)(2,1)S(1)} %subtract_convert_fusion, bf16[16,2048]{1,0:T(8,128)(2,1)S(1)} %collective-permute-done.7, bf16[4096,2048]{1,0:T(8,128)(2,1)} %copy-done), kind=kOutput, calls=%fused_computation.14 | convolution fusion | flops 4328521728 | bytes 21037056 | tf_op jit(solution)/shard_map/dot_general | solution.py:31
  278.9 9.2 %fusion.10 = f32[1,256,2048]{2,1,0:T(8,128)S(1)} fusion(bf16[4096,256]{1,0:T(8,128)(2,1)S(1)} %subtract_convert_fusion, bf16[16,2048]{1,0:T(8,128)(2,1)S(1)} %collective-permute-done.7, bf16[4096,2048]{1,0:T(8,128)(2,1)} %copy-done), kind=kOutput, calls=%fused_computation.13 | convolution fusion | flops 4328521728 | bytes 21037056 | tf_op jit(solution)/shard_map/dot_general | solution.py:31
  288.2 9.1 %fusion.16 = f32[1,256,2048]{2,1,0:T(8,128)} fusion(bf16[4096,256]{1,0:T(8,128)(2,1)S(1)} %subtract_convert_fusion, bf16[16,2048]{1,0:T(8,128)(2,1)S(1)} %collective-permute-done.7, bf16[4096,2048]{1,0:T(8,128)(2,1)} %copy-done), kind=kOutput, calls=%fused_computation.15 | convolution fusion | flops 4328521728 | bytes 21037056 | tf_op jit(solution)/shard_map/dot_general | solution.py:31
  297.3 5.0 %pad_maximum_fusion.2 = f32[4,256,2048]{2,1,0:T(8,128)} fusion(f32[1,256,2048]{2,1,0:T(8,128)} %fusion.16, f32[1,256,2048]{2,1,0:T(8,128)S(1)} %fusion.10, f32[1,256,2048]{2,1,0:T(8,128)S(1)} %fusion.13, f32[1,256,2048]{2,1,0:T(8,128)S(1)} %convolution_bitcast_fusion), kind=kLoop, calls=%fused_computation.11 | loop fusion | flops 6291456 | bytes 16777216 | tf_op jit(solution)/shard_map/stack | solution.py:39
  302.3 0.0 reduce-scatter.2.cloned.1.call-update
  302.3 142.1 %reduce-scatter.2.cloned.1.call-done = f32[4,256,512]{2,1,0:T(8,128)} async-done(((f32[4,256,2048]{2,1,0:T(8,128)}), f32[4,256,512]{2,1,0:T(8,128)}) %reduce-scatter.2.cloned.1.call-update) | async-done | bytes 2097168 | tf_op jit(solution)/shard_map/reduce_scatter | solution.py:40
  444.4 0.0 copy-done.12
  444.4 3.3 broadcast_multiply_fusion
  (9 shorter events, 0.0 us)
Async XLA Ops:
  6.5 437.8 %reduce-scatter.2.cloned.1.call-start = ((), (), s32[]{:S(2)}) async-start(), calls=%async_computation.1 | async-start | bytes 10485760 | tf_op jit(solution)/shard_map/reduce_scatter | solution.py:40
  25.3 26.4 %collective-permute-start = (bf16[4096,256]{1,0:T(8,128)(2,1)S(1)}, bf16[4096,256]{1,0:T(8,128)(2,1)S(1)}, u32[]{:S(2)}, u32[]{:S(2)}) collective-permute-start(bf16[4096,256]{1,0:T(8,128)(2,1)S(1)} %subtract_convert_fusion), channel_id=1, source_target_pairs={{0,1},{1,2},{2,3},{3,4},{4,5},{5,6},{6,7},{7,0},{8,9},{9,10},{10,1... | collective-permute-start | bytes 6291464 | tf_op jit(solution)/shard_map/ppermute | solution.py:24
  51.7 1.3 copy-start.2
  53.1 26.4 %collective-permute-start.1 = (bf16[4096,256]{1,0:T(8,128)(2,1)S(1)}, bf16[4096,256]{1,0:T(8,128)(2,1)S(1)}, u32[]{:S(2)}, u32[]{:S(2)}) collective-permute-start(bf16[4096,256]{1,0:T(8,128)(2,1)S(1)} %collective-permute-done), channel_id=1, source_target_pairs={{0,1},{1,2},{2,3},{3,4},{4,5},{5,6},{6,7},{7,0},{8,9},{9,10},{10,1... | collective-permute-start | bytes 6291464 | tf_op jit(solution)/shard_map/ppermute | solution.py:24
  79.4 1.4 copy-start.4
  80.8 26.4 %collective-permute-start.2 = (bf16[4096,256]{1,0:T(8,128)(2,1)S(1)}, bf16[4096,256]{1,0:T(8,128)(2,1)S(1)}, u32[]{:S(2)}, u32[]{:S(2)}) collective-permute-start(bf16[4096,256]{1,0:T(8,128)(2,1)S(1)} %collective-permute-done.1), channel_id=1, source_target_pairs={{0,1},{1,2},{2,3},{3,4},{4,5},{5,6},{6,7},{7,0},{8,9},{9,10},{10,1... | collective-permute-start | bytes 6291464 | tf_op jit(solution)/shard_map/ppermute | solution.py:24
  107.2 1.3 copy-start.6
  108.5 26.4 %collective-permute-start.3 = (bf16[4096,256]{1,0:T(8,128)(2,1)S(1)}, bf16[4096,256]{1,0:T(8,128)(2,1)S(1)}, u32[]{:S(2)}, u32[]{:S(2)}) collective-permute-start(bf16[4096,256]{1,0:T(8,128)(2,1)S(1)} %collective-permute-done.2), channel_id=1, source_target_pairs={{0,1},{1,2},{2,3},{3,4},{4,5},{5,6},{6,7},{7,0},{8,9},{9,10},{10,1... | collective-permute-start | bytes 6291464 | tf_op jit(solution)/shard_map/ppermute | solution.py:24
  134.8 1.3 copy-start.8
  136.1 26.4 %collective-permute-start.4 = (bf16[4096,256]{1,0:T(8,128)(2,1)S(1)}, bf16[4096,256]{1,0:T(8,128)(2,1)S(1)}, u32[]{:S(2)}, u32[]{:S(2)}) collective-permute-start(bf16[4096,256]{1,0:T(8,128)(2,1)S(1)} %collective-permute-done.3), channel_id=1, source_target_pairs={{0,1},{1,2},{2,3},{3,4},{4,5},{5,6},{6,7},{7,0},{8,9},{9,10},{10,1... | collective-permute-start | bytes 6291464 | tf_op jit(solution)/shard_map/ppermute | solution.py:24
  162.5 1.3 copy-start.10
  163.8 26.5 %collective-permute-start.5 = (bf16[4096,256]{1,0:T(8,128)(2,1)S(1)}, bf16[4096,256]{1,0:T(8,128)(2,1)}, u32[]{:S(2)}, u32[]{:S(2)}) collective-permute-start(bf16[4096,256]{1,0:T(8,128)(2,1)S(1)} %collective-permute-done.4), channel_id=1, source_target_pairs={{0,1},{1,2},{2,3},{3,4},{4,5},{5,6},{6,7},{7,0},{8,9},{9,10},{10,1... | collective-permute-start | bytes 6291464 | tf_op jit(solution)/shard_map/ppermute | solution.py:24
  190.3 26.7 %collective-permute-start.6 = (bf16[4096,256]{1,0:T(8,128)(2,1)}, bf16[4096,256]{1,0:T(8,128)(2,1)}, u32[]{:S(2)}, u32[]{:S(2)}) collective-permute-start(bf16[4096,256]{1,0:T(8,128)(2,1)} %collective-permute-done.5), channel_id=1, source_target_pairs={{0,1},{1,2},{2,3},{3,4},{4,5},{5,6},{6,7},{7,0},{8,9},{9,10},{10,1... | collective-permute-start | bytes 6291464 | tf_op jit(solution)/shard_map/ppermute | solution.py:24
  190.3 39.2 %copy-start.7 = (bf16[4096,256]{1,0:T(8,128)(2,1)S(1)}, bf16[4096,256]{1,0:T(8,128)(2,1)}, u32[]{:S(2)}) copy-start(bf16[4096,256]{1,0:T(8,128)(2,1)} %copy-done.6) | copy-start | bytes 6291460
  190.3 40.7 %copy-start.5 = (bf16[4096,256]{1,0:T(8,128)(2,1)S(1)}, bf16[4096,256]{1,0:T(8,128)(2,1)}, u32[]{:S(2)}) copy-start(bf16[4096,256]{1,0:T(8,128)(2,1)} %copy-done.4) | copy-start | bytes 6291460
  190.3 42.1 %copy-start.3 = (bf16[4096,256]{1,0:T(8,128)(2,1)S(1)}, bf16[4096,256]{1,0:T(8,128)(2,1)}, u32[]{:S(2)}) copy-start(bf16[4096,256]{1,0:T(8,128)(2,1)} %copy-done.2) | copy-start | bytes 6291460
  190.3 43.6 %copy-start.1 = (f32[4096,256]{1,0:T(8,128)S(1)}, f32[4096,256]{1,0:T(8,128)}, u32[]{:S(2)}) copy-start(f32[4096,256]{1,0:T(8,128)} %param.2) | copy-start | bytes 12582916
  226.2 15.5 %copy-start.11 = (bf16[4096,256]{1,0:T(8,128)(2,1)S(1)}, bf16[4096,256]{1,0:T(8,128)(2,1)}, u32[]{:S(2)}) copy-start(bf16[4096,256]{1,0:T(8,128)(2,1)} %copy-done.10) | copy-start | bytes 6291460
  229.5 13.8 %copy-start.9 = (bf16[4096,256]{1,0:T(8,128)(2,1)S(1)}, bf16[4096,256]{1,0:T(8,128)(2,1)}, u32[]{:S(2)}) copy-start(bf16[4096,256]{1,0:T(8,128)(2,1)} %copy-done.8) | copy-start | bytes 6291460
  259.4 5.7 %copy-start = (bf16[4096,2048]{1,0:T(8,128)(2,1)}, bf16[4096,2048]{1,0:T(8,128)(2,1)S(1)}, u32[]{:S(2)}) copy-start(bf16[4096,2048]{1,0:T(8,128)(2,1)S(1)} %constant_dynamic-slice_fusion.1) | copy-start | bytes 50331652
  260.4 9.3 %collective-permute-start.7 = (bf16[16,2048]{1,0:T(8,128)(2,1)S(1)}, bf16[16,2048]{1,0:T(8,128)(2,1)S(1)}, u32[]{:S(2)}, u32[]{:S(2)}) collective-permute-start(bf16[16,2048]{1,0:T(8,128)(2,1)S(1)} %constant_dynamic-slice_fusion), channel_id=1, source_target_pairs={{8,0},{16,8},{24,16},{9,1},{17,9},{25,17},{10,2},{18,10},{26,18},{... | collective-permute-start | bytes 196616 | tf_op jit(solution)/shard_map/ppermute | solution.py:13
  297.3 147.1 %copy-start.12 = (f32[4]{0:T(128)S(1)}, f32[4]{0:T(128)}, u32[]{:S(2)}) copy-start(f32[4]{0:T(128)} %constant.43) | copy-start | bytes 52
Sparse Core Ops, SparseCore 0:
  302.4 141.8 reduce-scatter.1
